TPU v7x, 32 devices: a whole 2x2x4 slice. The times are simulated.
32 devices in a mesh: clip: 2 (over y), height: 4 (over z), head: 4 (over x, core).
Axes of the slice: x: 2, y: 2, z: 4, core: 2. Of those that a mesh axis runs over, the one named last changes fastest.
Arguments:
- tokens: bfloat16 [8, 192, 5120], P(('clip', 'height'), None, 'head'), parts along dimension 0, may hold values from -6 to 6
- in_sign: int32 [5120], replicated, may hold values from 0 to 1
- qkv_codes: int32 [640, 3, 3072], P(None, None, 'head'), may hold values from 0 to 65535
- qkv_scale: float32 [3, 3072], P(None, 'head'), may hold values from 0.3 to 3
- qkv_sign: int32 [3, 3072], P(None, 'head'), may hold values from 0 to 1
- windows: int32 [8, 3, 27], P(('clip', 'height')), parts along dimension 0, may hold values from 0 to 11, as said below
- oin_sign: int32 [3072], P('head'), may hold values from 0 to 1
- out_codes: int32 [384, 5120], P('head'), may hold values from 0 to 65535
- out_scale: float32 [5120], replicated, may hold values from 2 to 20
- out_sign: int32 [5120], replicated, may hold values from 0 to 1
Outputs:
- attention_out: bfloat16 [8, 192, 5120], P(('clip', 'height'), 'head'), parts along dimension 0
There are 2 independent parts, one for each index of `clip`. A program takes and returns all parts, laid end to end along the dimension named above; an argument that names none is the same for every part. Nothing has to cross between parts.
Inputs may be any that keep to these rules, and one draw needn't show every extreme that they name: `windows`: each row lists the query tile itself and 26 further entries, each one of the 27 tiles of the 3 x 3 x 3 block of tiles centred on the query tile (each of the three coordinates clipped into the grid of 1 x 4 x 3 tiles); entries may repeat and appear in any order.
All inputs are finite; a program needn't handle non-finite values.
Results may differ from a plain program's by a relative error of at most 0.015.
Values may be sent and summed in bfloat16 or wider, within the bound.
A program may use at most 128 MiB of HBM per device.

v0:
```python
import functools

import jax
import jax.numpy as jnp
import numpy as np
from jax import lax
from jax.experimental import pallas as pl
from jax.experimental.pallas import tpu as pltpu
from jax.sharding import PartitionSpec as P

HD = 128
HAD = 128
TILE = 64
HROWS = 4
PLANES = 8
GROUP = HAD // PLANES
EPSILON = 1e-06
MESH = pl.DeviceIdType.MESH
VLIMIT = 60 * 1024 * 1024


def sylvester(order_size):
    matrix_now = np.ones((1, 1), np.float32)
    seed_pair = np.array([[1.0, 1.0], [1.0, -1.0]], np.float32)
    while matrix_now.shape[0] < order_size:
        matrix_now = np.kron(matrix_now, seed_pair)
    return matrix_now


ORDER = np.array([8 * i + k for k in range(PLANES) for i in range(GROUP)])
PLANE_POWER = np.array([4.0**k for k in range(PLANES) for _ in range(GROUP)], np.float32)


def plain_matrix():
    return jnp.asarray(sylvester(HAD), jnp.bfloat16)


def plane_matrix():
    return jnp.asarray(sylvester(HAD)[:, ORDER], jnp.bfloat16)


def plane_scale():
    return jnp.asarray((HAD**-0.5 / PLANE_POWER)[None, :], jnp.float32)


def plane_power():
    return jnp.asarray(PLANE_POWER[None, :], jnp.float32)


def signed(sign_bits):
    return (2 * sign_bits - 1).astype(jnp.float32)


def dot(left, right):
    return jnp.dot(left, right, preferred_element_type=jnp.float32)


def rotate_split(block, matrix):
    high = block.astype(jnp.bfloat16)
    low = (block - high.astype(jnp.float32)).astype(jnp.bfloat16)
    return (dot(high, matrix) + dot(low, matrix)) * HAD**-0.5


def unpack_block(words):
    planes = [(words & (3 << (2 * k))).astype(jnp.float32).astype(jnp.bfloat16) for k in range(PLANES)]
    pieces = []
    for block in range(words.shape[0] // GROUP):
        for k in range(PLANES):
            pieces.append(planes[k][block * GROUP : (block + 1) * GROUP])
    return jnp.concatenate(pieces, axis=0)


def row_sums(rows, power):
    total = None
    for block in range(rows.shape[1] // HAD):
        part = rows[:, block * HAD : (block + 1) * HAD].astype(jnp.float32) * power
        total = part if total is None else total + part
    return jnp.sum(total, axis=1, keepdims=True)


def layer_kernel(
    n, peers, distances, cols, gcols,
    x_ref, insign_ref, qscale_ref, qsign_ref, listed_ref, osign_ref, oscale_ref, outsign_ref,
    plane_mat_ref, mat_ref, pscale_ref, power_ref, codes_ref, ocodes_ref,
    out_ref,
    turned, words, weights, acc, offset, qkv, near, owords, oweights, gathered, totals,
    rotated, ooffset, lines, part, word_sem, oword_sem, halo_send, halo_recv, *scratch,
):
    me = lax.axis_index("head")
    row = lax.axis_index("height")
    rows, width = x_ref.shape
    count = words.shape[0]
    per_part = count // 3
    per_chunk = cols // HD
    local = per_part * cols
    depth = width // PLANES
    qtiles = rows // TILE
    groups = part.shape[0]
    share = rows // n
    slots = len(distances)

    def fetch(j):
        return pltpu.make_async_copy(
            codes_ref.at[(j // per_part + 1) % 3, :, pl.ds(pl.multiple_of(j % per_part * cols, HD), cols)],
            words.at[j],
            word_sem.at[j],
        )

    for j in range(count):
        fetch(j).start()
    fetch_out = pltpu.make_async_copy(ocodes_ref, owords, oword_sem)
    fetch_out.start()

    barrier = pltpu.get_barrier_semaphore()
    if n == 4:
        partner = me + 1 - 2 * (me % 2)
        across = (me + 2) % 4
        diagonal = (partner + 2) % 4
        head_peers = [partner, across]
        early, late = [me, partner], [across, diagonal]
    else:
        head_peers = [(me + p) % n for p in range(1, n)]
        early, late = [me], head_peers
    gives = [jnp.logical_and(row + d >= 0, row + d < peers) for d in distances]
    takes = [jnp.logical_and(row - d >= 0, row - d < peers) for d in distances]
    for peer in head_peers:
        pl.semaphore_signal(barrier, inc=1, device_id={"head": peer}, device_id_type=MESH)
    greeted = jnp.int32(len(head_peers))
    for slot, distance in enumerate(distances):

        @pl.when(gives[slot])
        def _():
            pl.semaphore_signal(
                barrier, inc=1, device_id={"height": row + distance}, device_id_type=MESH
            )

        greeted = greeted + jnp.where(gives[slot], 1, 0)

    for block in range(width // HAD):
        lanes = slice(block * HAD, (block + 1) * HAD)
        spun = dot(x_ref[:, lanes] * insign_ref[:, lanes].astype(jnp.bfloat16), plane_mat_ref[...])
        turned[me, :, lanes] = (spun * pscale_ref[...]).astype(jnp.bfloat16)
    for j in range(count):
        source = (j // per_part + 1) % 3
        spots = slice(j % per_part * cols, (j % per_part + 1) * cols)
        for place, ref in enumerate((qscale_ref, qsign_ref)):
            line = jnp.broadcast_to(ref[source : source + 1, spots], (8, cols))
            lines[j, 8 * place : 8 * place + 8, :] = line
    pl.semaphore_wait(barrier, greeted)

    def head_copy(src, dst, send, recv, peer):
        return pltpu.make_async_remote_copy(
            src, dst, send, recv, device_id={"head": peer}, device_id_type=MESH
        )

    def unpack(j):
        fetch(j).wait()
        for shard in range(n):
            weights[j, shard] = unpack_block(words[j, shard * depth : (shard + 1) * depth, :])
        total = dot(turned[early[0]], weights[j, early[0]])
        for shard in early[1:]:
            total = total + dot(turned[shard], weights[j, shard])
        acc[j] = total

    if n == 4:
        a_send, a_recv, f_send, f_recv, b_send, b_recv = scratch[:6]
        scratch = scratch[6:]
        chunks = a_send.shape[0]
        step = rows // chunks

        def piece(slot, c):
            return turned.at[slot, pl.ds(c * step, step), :]

        crossing = [
            head_copy(piece(me, c), piece(me, c), a_send.at[c], a_recv.at[c], across)
            for c in range(chunks)
        ]
        relays = [
            head_copy(piece(across, c), piece(across, c), f_send.at[c], f_recv.at[c], partner)
            for c in range(chunks)
        ]
        for copy in crossing:
            copy.start()
        beside = head_copy(turned.at[me], turned.at[me], b_send, b_recv, partner)
        beside.start()
        beside.wait_recv()
        done = 0
        for c in range(chunks):
            upto = count * (c + 1) // chunks

            @pl.loop(done, upto)
            def _(j):
                unpack(j)

            done = upto
            crossing[c].wait_recv()
            relays[c].start()
        for copy in relays:
            copy.wait_recv()
        sent = crossing + relays + [beside]
    else:
        g_send, g_recv = scratch[:2]
        scratch = scratch[2:]
        sent = [
            head_copy(turned.at[me], turned.at[me], g_send.at[p], g_recv.at[p], peer)
            for p, peer in enumerate(head_peers)
        ]
        for copy in sent:
            copy.start()

        @pl.loop(0, count)
        def _(j):
            unpack(j)

        for copy in sent:
            copy.wait_recv()

    total = jnp.zeros((rows, 1), jnp.float32)
    for shard in range(n):
        total = total + row_sums(turned[shard], power_ref[...])
    offset[...] = jnp.broadcast_to(1.5 * total, offset.shape)

    def finish(j):
        result = acc[j]
        for shard in late:
            result = result + dot(turned[shard], weights[j, shard])
        source = (j // per_part + 1) % 3
        for head in range(per_chunk):
            lanes = slice(head * HD, (head + 1) * HD)
            block = (result[:, lanes] - offset[...]) * lines[j, 0:1, lanes]
            block = rotate_split(block, mat_ref[...]) * lines[j, 8:9, lanes]
            mean = jnp.mean(block * block, axis=-1, keepdims=True)
            divisor = jnp.where(source < 2, jnp.sqrt(mean + EPSILON), 1.0)
            qkv[j, :, lanes] = (block / divisor).astype(jnp.bfloat16)

    def halo_copy(slot, j):
        return pltpu.make_async_remote_copy(
            qkv.at[j], near.at[slot, j], halo_send.at[slot, j], halo_recv.at[slot, j],
            device_id={"height": row + distances[slot]}, device_id_type=MESH,
        )

    @pl.loop(0, 2 * per_part)
    def _(j):
        finish(j)
        for slot in range(slots):

            @pl.when(gives[slot])
            def _():
                halo_copy(slot, j).start()

    for slot in range(slots):

        @pl.when(jnp.logical_not(takes[slot]))
        def _():
            near[slot] = jnp.zeros(near.shape[1:], near.dtype)

    @pl.loop(2 * per_part, count)
    def _(j):
        finish(j)

    def mask_of(first_tile):
        ids = lax.broadcasted_iota(jnp.int32, (8, rows), 1) // TILE + first_tile
        stack = []
        for tile in range(qtiles):
            hit = ids == listed_ref[0, tile, 0]
            for entry in range(1, listed_ref.shape[2]):
                hit = jnp.logical_or(hit, ids == listed_ref[0, tile, entry])
            stack.extend([jnp.where(hit, 1.0, 0.0)] * (TILE // 8))
        return jnp.concatenate(stack, axis=0)

    def attend(queries, keys, values, mask):
        score = lax.dot_general(
            queries, keys, (((1,), (1,)), ((), ())), preferred_element_type=jnp.float32
        )
        weight = jnp.exp(score * HD**-0.5) * mask
        return dot(weight.astype(jnp.bfloat16), values), jnp.sum(weight, axis=-1, keepdims=True)

    own_mask = mask_of(row * qtiles)
    near_masks = [mask_of((row - d) * qtiles) for d in distances]
    for head in range(local // HD):
        chunk, lanes = head // per_chunk, slice(head % per_chunk * HD, (head % per_chunk + 1) * HD)
        found, sums = attend(
            qkv[2 * per_part + chunk, :, lanes], qkv[chunk, :, lanes],
            qkv[per_part + chunk, :, lanes], own_mask,
        )
        gathered[head] = found
        totals[head] = jnp.broadcast_to(sums, found.shape)

    fetch_out.wait()

    @pl.loop(0, groups)
    def _(g):
        spots = pl.ds(pl.multiple_of(g * gcols, HD), gcols)
        oweights[g] = unpack_block(owords[:, spots])

    for slot in range(slots):

        @pl.when(takes[slot])
        def _():
            for j in range(2 * per_part):
                halo_copy(slot, j).wait_recv()

    for head in range(local // HD):
        chunk, lanes = head // per_chunk, slice(head % per_chunk * HD, (head % per_chunk + 1) * HD)
        found, sums = gathered[head], totals[head]
        for slot in range(slots):
            more, more_sums = attend(
                qkv[2 * per_part + chunk, :, lanes], near[slot, chunk, :, lanes],
                near[slot, per_part + chunk, :, lanes], near_masks[slot],
            )
            found, sums = found + more, sums + more_sums
        attended = (found / sums).astype(jnp.bfloat16)
        spots = slice(head * HD, (head + 1) * HD)
        spun = dot(attended * osign_ref[:, spots].astype(jnp.bfloat16), plane_mat_ref[...])
        rotated[:, spots] = (spun * pscale_ref[...]).astype(jnp.bfloat16)
    ooffset[...] = jnp.broadcast_to(1.5 * row_sums(rotated[...], power_ref[...]), ooffset.shape)

    def produce(g):
        result = dot(rotated[...], oweights[g])
        for block in range(gcols // HAD):
            lanes = slice(block * HAD, (block + 1) * HAD)
            spots = slice(g * gcols + block * HAD, g * gcols + (block + 1) * HAD)
            value = (result[:, lanes] - ooffset[...]) * oscale_ref[:, spots]
            part[g, :, :, lanes] = value.reshape(n, share, HAD).astype(jnp.bfloat16)

    def conclude(g, terms):
        for block in range(gcols // HAD):
            lanes = slice(block * HAD, (block + 1) * HAD)
            spots = slice(g * gcols + block * HAD, g * gcols + (block + 1) * HAD)
            total = part[g, me, :, lanes].astype(jnp.float32)
            for term in terms:
                total = total + term[:, lanes].astype(jnp.float32)
            spun = rotate_split(total, mat_ref[...]) * outsign_ref[:, spots]
            out_ref[:, spots] = spun.astype(jnp.bfloat16)

    if n == 4:
        staged, flank, summed, crossed, p_send, p_recv, q_send, q_recv, x_send, x_recv = scratch
        first = [
            head_copy(part.at[g, diagonal], staged.at[g], p_send.at[g], p_recv.at[g], partner)
            for g in range(groups)
        ]
        second = [
            head_copy(part.at[g, partner], flank.at[g], q_send.at[g], q_recv.at[g], partner)
            for g in range(groups)
        ]
        third = [
            head_copy(summed.at[g], crossed.at[g], x_send.at[g], x_recv.at[g], across)
            for g in range(groups)
        ]

        def relay(g):
            first[g].wait_recv()
            summed[g] = (
                part[g, across].astype(jnp.float32) + staged[g].astype(jnp.float32)
            ).astype(jnp.bfloat16)
            third[g].start()

        for g in range(groups):
            produce(g)
            first[g].start()
            second[g].start()
            if g > 0:
                relay(g - 1)
        relay(groups - 1)
        for g in range(groups):
            second[g].wait_recv()
            third[g].wait_recv()
            conclude(g, [flank[g], crossed[g]])
        sent = sent + first + second + third
    else:
        landed, r_send, r_recv = scratch
        moves = []
        for g in range(groups):
            produce(g)
            move = [
                head_copy(part.at[g, peer], landed.at[p, g], r_send.at[p, g], r_recv.at[p, g], peer)
                for p, peer in enumerate(head_peers)
            ]
            for copy in move:
                copy.start()
            moves.append(move)
        for g in range(groups):
            for copy in moves[g]:
                copy.wait_recv()
            conclude(g, [landed[p, g] for p in range(n - 1)])
        sent = sent + [copy for move in moves for copy in move]

    for copy in sent:
        copy.wait_send()
    for slot in range(slots):

        @pl.when(gives[slot])
        def _():
            for j in range(2 * per_part):
                halo_copy(slot, j).wait_send()


def on_device(
    n,
    peers,
    tokens,
    in_sign,
    qkv_codes,
    qkv_scale,
    qkv_sign,
    windows,
    oin_sign,
    out_codes,
    out_scale,
    out_sign,
):
    own = tokens[0]
    rows, width = own.shape
    model = width * n
    local = qkv_scale.shape[1]
    features = out_codes.shape[1]
    place = lax.axis_index("head")
    own_sign = lax.dynamic_slice_in_dim(in_sign, place * width, width, 0)
    reach = (1,) if peers <= HROWS else (1, HROWS - 1, HROWS, HROWS + 1)
    distances = tuple(d for r in reach if r < peers for d in (r, -r))
    slots = len(distances)
    cols = 256 if local % 256 == 0 else HD
    count = 3 * local // cols
    per_part = count // 3
    inner = qkv_codes.shape[0]
    gcols = 1024 if features % 1024 == 0 else HD
    groups = features // gcols
    share = rows // n
    chunks = 4
    dma = pltpu.SemaphoreType.DMA
    grouped = pltpu.VMEM((groups, share, gcols), jnp.bfloat16)
    if n == 4:
        tail = [dma((chunks,))] * 4 + [dma] * 2 + [grouped] * 4 + [dma((groups,))] * 6
    else:
        tail = [dma((n - 1,))] * 2
        tail += [pltpu.VMEM((n - 1, groups, share, gcols), jnp.bfloat16)]
        tail += [dma((n - 1, groups))] * 2
    vmem = pl.BlockSpec(memory_space=pltpu.VMEM)
    anywhere = pl.BlockSpec(memory_space=pl.ANY)
    smem = pl.BlockSpec(memory_space=pltpu.SMEM)
    result = pl.pallas_call(
        functools.partial(layer_kernel, n, peers, distances, cols, gcols),
        name="layer",
        out_shape=jax.ShapeDtypeStruct((share, features), jnp.bfloat16),
        in_specs=[vmem] * 4 + [smem] + [vmem] * 7 + [anywhere] * 2,
        out_specs=vmem,
        scratch_shapes=[
            pltpu.VMEM((n, rows, width), jnp.bfloat16),
            pltpu.VMEM((count, inner, cols), jnp.int32),
            pltpu.VMEM((count, n, width, cols), jnp.bfloat16),
            pltpu.VMEM((count, rows, cols), jnp.float32),
            pltpu.VMEM((rows, HD), jnp.float32),
            pltpu.VMEM((count, rows, cols), jnp.bfloat16),
            pltpu.VMEM((slots, 2 * per_part, rows, cols), jnp.bfloat16),
            pltpu.VMEM(out_codes.shape, jnp.int32),
            pltpu.VMEM((groups, local, gcols), jnp.bfloat16),
            pltpu.VMEM((local // HD, rows, HD), jnp.float32),
            pltpu.VMEM((local // HD, rows, HD), jnp.float32),
            pltpu.VMEM((rows, local), jnp.bfloat16),
            pltpu.VMEM((rows, HD), jnp.float32),
            pltpu.VMEM((count, 16, cols), jnp.float32),
            pltpu.VMEM((groups, n, share, gcols), jnp.bfloat16),
            dma((count,)),
            dma,
            dma((slots, 2 * per_part)),
            dma((slots, 2 * per_part)),
        ]
        + tail,
        compiler_params=pltpu.CompilerParams(
            collective_id=0, has_side_effects=True, vmem_limit_bytes=VLIMIT
        ),
    )(
        own,
        signed(own_sign)[None],
        qkv_scale * model**-0.5,
        signed(qkv_sign),
        windows,
        signed(oin_sign)[None],
        (out_scale * (local * n) ** -0.5)[None],
        signed(out_sign)[None],
        plane_matrix(),
        plain_matrix(),
        plane_scale(),
        plane_power(),
        jnp.transpose(qkv_codes, (1, 0, 2)),
        out_codes,
    )
    return result[None]


def solution(mesh):
    n = mesh.shape["head"]
    peers = mesh.shape["height"]
    return jax.shard_map(
        functools.partial(on_device, n, peers),
        mesh=mesh,
        in_specs=(
            P(("clip", "height"), None, "head"),
            P(),
            P(None, None, "head"),
            P(None, "head"),
            P(None, "head"),
            P(("clip", "height"), None, None),
            P("head"),
            P("head", None),
            P(),
            P(),
        ),
        out_specs=P(("clip", "height"), "head", None),
        check_vma=False,
    )
```

profile of v0, /device:TPU:0, one launch (start us, length us, event | category | flops | bytes accessed | tf_op | source)
XLA Modules:
  0.0 63.4 jit_solution(4634914846702699060)
XLA Ops:
  0.0 1.3 %copy.15.listed_ref = s32[1,3,27]{2,1,0:T(4,128)} copy(s32[1,3,27]{2,0,1:T(1,128)} %param.19) | data formatting | bytes 648 | tf_op args[5]
  1.3 0.7 %add_convert_fusion.3 = f32[768]{0:T(1024)S(1)} fusion(s32[768]{0:T(1024)} %param.20), kind=kLoop, calls=%fused_computation.5 | loop fusion | flops 2304 | bytes 6144 | tf_op jit(solution)/shard_map/convert_element_type | solution.py:51
  2.0 0.6 broadcast_in_dim.16.osign_ref
  2.6 0.8 %add_convert_fusion.2 = f32[1280]{0:T(1024)S(1)} fusion(s32[5120]{0:T(1024)} %param.15, s32[]{:T(128)S(6)} %select_n.3), kind=kLoop, calls=%fused_computation.3 | loop fusion | flops 3840 | bytes 10244 | tf_op jit(solution)/shard_map/convert_element_type | solution.py:51
  3.3 0.6 broadcast_in_dim.15.insign_ref
  3.9 1.3 %broadcast_multiply_fusion.1.qscale_ref = f32[3,768]{1,0:T(4,128)} fusion(f32[3,768]{1,0:T(4,128)} %param.17), kind=kLoop, calls=%fused_computation.4 | loop fusion | flops 2304 | bytes 18432 | tf_op jit(solution)/shard_map/mul | solution.py:475
  5.3 1.3 %add_convert_fusion.1.qsign_ref = f32[3,768]{1,0:T(4,128)} fusion(s32[3,768]{1,0:T(4,128)} %param.18), kind=kLoop, calls=%fused_computation.1 | loop fusion | flops 6912 | bytes 18432 | tf_op jit(solution)/shard_map/convert_element_type | solution.py:51
  6.6 1.3 %broadcast_multiply_fusion = f32[5120]{0:T(1024)} fusion(f32[5120]{0:T(1024)} %param.22), kind=kLoop, calls=%fused_computation.2 | loop fusion | flops 5120 | bytes 40960 | tf_op jit(solution)/shard_map/mul | solution.py:479
  7.9 1.3 %add_convert_fusion = f32[5120]{0:T(1024)} fusion(s32[5120]{0:T(1024)} %param.23), kind=kLoop, calls=%fused_computation | loop fusion | flops 15360 | bytes 40960 | tf_op jit(solution)/shard_map/convert_element_type | solution.py:51
  9.2 52.3 %layer.1 = bf16[48,5120]{1,0:T(8,128)(2,1)} custom-call(bf16[192,1280]{1,0:T(8,128)(2,1)} %bitcast.7, f32[1,1280]{1,0:T(1,128)} %broadcast_in_dim.15.insign_ref, f32[3,768]{1,0:T(4,128)} %broadcast_multiply_fusion.1.qscale_ref, f32[3,768]{1,0:T(4,128)} %add_convert_fusion.1.qsign_ref, s32[1,3,27]{2,1,0:T(4,128)} %copy.15.listed_ref, ...), custom_call_target="tpu_custom_call" | custom-call | tf_op jit(solution)/shard_map/layer/pallas_call | solution.py:441
  61.5 1.8 %copy.17 = bf16[1,48,5120]{2,1,0:T(8,128)(2,1)} copy(bf16[1,48,5120]{2,1,0:T(8,128)(2,1)} %bitcast.6) | data formatting | bytes 983040
where the time goes:
time: 63.9 us; the launch traced here: 63.4 us
  Pallas kernels  52.3 us (82%)
  other arithmetic  6.74 us (11%)
  local copies, waits for them, and re-layouts  4.31 us (7%)
    pallas_call x1, Pallas kernels, on_device(): pl.pallas_call(functools.partial(layer_kernel, n, peers, distances, cols,...  52.3 us
    convert_element_type x4, other arithmetic, signed(): return (2 * sign_bits - 1).astype(jnp.float32)  4.1 us
    unnamed x2, local copies, waits for them, and re-layouts  3.12 us
    mul x1, other arithmetic, on_device(): out_scale * (local * n) ** (-0.5)  1.34 us
    mul x1, other arithmetic, on_device(): qkv_scale * model ** (-0.5)  1.31 us

commit v1 on v0

--- a/solution.py
+++ b/solution.py
@@ -80,11 +80,11 @@
 
 def layer_kernel(
     n, peers, distances, cols, gcols,
-    x_ref, insign_ref, qscale_ref, qsign_ref, listed_ref, osign_ref, oscale_ref, outsign_ref,
+    x_ref, insigns_ref, qscale_ref, qsign_ref, listed_ref, osign_ref, oscale_ref, outsign_ref,
     plane_mat_ref, mat_ref, pscale_ref, power_ref, codes_ref, ocodes_ref,
     out_ref,
     turned, words, weights, acc, offset, qkv, near, owords, oweights, gathered, totals,
-    rotated, ooffset, lines, part, word_sem, oword_sem, halo_send, halo_recv, *scratch,
+    rotated, ooffset, lines, insigns, part, word_sem, oword_sem, halo_send, halo_recv, *scratch,
 ):
     me = lax.axis_index("head")
     row = lax.axis_index("height")
@@ -136,16 +136,22 @@
 
         greeted = greeted + jnp.where(gives[slot], 1, 0)
 
+    for shard in range(n):
+        for block in range(width // HAD):
+            lanes = slice(block * HAD, (block + 1) * HAD)
+            line = signed(insigns_ref[shard * width + block * HAD : shard * width + (block + 1) * HAD])
+            insigns[shard, :, lanes] = jnp.broadcast_to(line[None, :], (8, HAD))
     for block in range(width // HAD):
         lanes = slice(block * HAD, (block + 1) * HAD)
-        spun = dot(x_ref[:, lanes] * insign_ref[:, lanes].astype(jnp.bfloat16), plane_mat_ref[...])
+        spun = dot(x_ref[:, lanes] * insigns[me, 0:1, lanes].astype(jnp.bfloat16), plane_mat_ref[...])
         turned[me, :, lanes] = (spun * pscale_ref[...]).astype(jnp.bfloat16)
     for j in range(count):
         source = (j // per_part + 1) % 3
         spots = slice(j % per_part * cols, (j % per_part + 1) * cols)
-        for place, ref in enumerate((qscale_ref, qsign_ref)):
-            line = jnp.broadcast_to(ref[source : source + 1, spots], (8, cols))
-            lines[j, 8 * place : 8 * place + 8, :] = line
+        scale = qscale_ref[source : source + 1, spots] * (width * n) ** -0.5
+        sign = signed(qsign_ref[source : source + 1, spots])
+        lines[j, 0:8, :] = jnp.broadcast_to(scale, (8, cols))
+        lines[j, 8:16, :] = jnp.broadcast_to(sign, (8, cols))
     pl.semaphore_wait(barrier, greeted)
 
     def head_copy(src, dst, send, recv, peer):
@@ -262,9 +268,9 @@
         ids = lax.broadcasted_iota(jnp.int32, (8, rows), 1) // TILE + first_tile
         stack = []
         for tile in range(qtiles):
-            hit = ids == listed_ref[0, tile, 0]
+            hit = ids == listed_ref[tile, 0, 0]
             for entry in range(1, listed_ref.shape[2]):
-                hit = jnp.logical_or(hit, ids == listed_ref[0, tile, entry])
+                hit = jnp.logical_or(hit, ids == listed_ref[tile, 0, entry])
             stack.extend([jnp.where(hit, 1.0, 0.0)] * (TILE // 8))
         return jnp.concatenate(stack, axis=0)
 
@@ -311,7 +317,7 @@
             found, sums = found + more, sums + more_sums
         attended = (found / sums).astype(jnp.bfloat16)
         spots = slice(head * HD, (head + 1) * HD)
-        spun = dot(attended * osign_ref[:, spots].astype(jnp.bfloat16), plane_mat_ref[...])
+        spun = dot(attended * signed(osign_ref[spots])[None, :].astype(jnp.bfloat16), plane_mat_ref[...])
         rotated[:, spots] = (spun * pscale_ref[...]).astype(jnp.bfloat16)
     ooffset[...] = jnp.broadcast_to(1.5 * row_sums(rotated[...], power_ref[...]), ooffset.shape)
 
@@ -320,7 +326,7 @@
         for block in range(gcols // HAD):
             lanes = slice(block * HAD, (block + 1) * HAD)
             spots = slice(g * gcols + block * HAD, g * gcols + (block + 1) * HAD)
-            value = (result[:, lanes] - ooffset[...]) * oscale_ref[:, spots]
+            value = (result[:, lanes] - ooffset[...]) * (oscale_ref[spots] * (local * n) ** -0.5)[None, :]
             part[g, :, :, lanes] = value.reshape(n, share, HAD).astype(jnp.bfloat16)
 
     def conclude(g, terms):
@@ -330,7 +336,7 @@
             total = part[g, me, :, lanes].astype(jnp.float32)
             for term in terms:
                 total = total + term[:, lanes].astype(jnp.float32)
-            spun = rotate_split(total, mat_ref[...]) * outsign_ref[:, spots]
+            spun = rotate_split(total, mat_ref[...]) * signed(outsign_ref[spots])[None, :]
             out_ref[:, spots] = spun.astype(jnp.bfloat16)
 
     if n == 4:
@@ -411,11 +417,8 @@
 ):
     own = tokens[0]
     rows, width = own.shape
-    model = width * n
     local = qkv_scale.shape[1]
     features = out_codes.shape[1]
-    place = lax.axis_index("head")
-    own_sign = lax.dynamic_slice_in_dim(in_sign, place * width, width, 0)
     reach = (1,) if peers <= HROWS else (1, HROWS - 1, HROWS, HROWS + 1)
     distances = tuple(d for r in reach if r < peers for d in (r, -r))
     slots = len(distances)
@@ -459,6 +462,7 @@
             pltpu.VMEM((rows, local), jnp.bfloat16),
             pltpu.VMEM((rows, HD), jnp.float32),
             pltpu.VMEM((count, 16, cols), jnp.float32),
+            pltpu.VMEM((n, 8, width), jnp.float32),
             pltpu.VMEM((groups, n, share, gcols), jnp.bfloat16),
             dma((count,)),
             dma,
@@ -471,13 +475,13 @@
         ),
     )(
         own,
-        signed(own_sign)[None],
-        qkv_scale * model**-0.5,
-        signed(qkv_sign),
-        windows,
-        signed(oin_sign)[None],
-        (out_scale * (local * n) ** -0.5)[None],
-        signed(out_sign)[None],
+        in_sign,
+        qkv_scale,
+        qkv_sign,
+        jnp.transpose(windows, (1, 0, 2)),
+        oin_sign,
+        out_scale,
+        out_sign,
         plane_matrix(),
         plain_matrix(),
         plane_scale(),

time: 63.9 us -> 54.3 us (0.85)
  other arithmetic: 6.74 us -> 0 us
  local copies, waits for them, and re-layouts: 4.31 us -> 1.84 us
    convert_element_type x4 -> x0, other arithmetic: 4.1 us -> none  [signed(): return (2 * sign_bits - 1).astype(jnp.float32)]
    mul x2 -> x0, other arithmetic: 2.64 us -> none  [the longest x1 1.34 us: on_device(): out_scale * (local * n) ** (-0.5)]
    unnamed x2 -> x1, local copies, waits for them, and re-layouts: 3.12 us -> 1.84 us
    broadcast_in_dim x2 -> x0, local copies, waits for them, and re-layouts: 1.19 us -> none  [the longest x1 0.6 us: on_device(): signed(own_sign)[None]]
where the time goes in v1:
time: 54.3 us; the launch traced here: 54.2 us
  Pallas kernels  52.3 us (96%)
  local copies, waits for them, and re-layouts  1.84 us (3%)
    pallas_call x1, Pallas kernels, on_device(): pl.pallas_call(functools.partial(layer_kernel, n, peers, distances, cols,...  52.3 us
    unnamed x1, local copies, waits for them, and re-layouts  1.84 us

profile of v1, /device:TPU:0, one launch (start us, length us, event | category | flops | bytes accessed | tf_op | source)
XLA Modules:
  0.0 54.2 jit_solution(4269595573084746512)
XLA Ops:
  0.0 52.3 %layer.1 = bf16[48,5120]{1,0:T(8,128)(2,1)} custom-call(bf16[192,1280]{1,0:T(8,128)(2,1)} %bitcast.6, s32[5120]{0:T(1024)} %insigns_ref.1, f32[3,768]{1,0:T(4,128)} %qscale_ref.1, s32[3,768]{1,0:T(4,128)} %qsign_ref.1, s32[3,1,27]{2,1,0:T(1,128)} %bitcast.7, s32[768]{0:T(1024)} %osign_ref.1, f32[5120]{0:T(1024)} %oscale_ref.1, s32[5120]{0:T(1024)} %outsign_ref.1, ...), custom_call_target="tpu_custom_call" | custom-call | tf_op jit(solution)/shard_map/layer/pallas_call | solution.py:444
  52.3 1.8 %copy.16 = bf16[1,48,5120]{2,1,0:T(8,128)(2,1)} copy(bf16[1,48,5120]{2,1,0:T(8,128)(2,1)} %bitcast.5) | data formatting | bytes 983040

commit v2 on v1

--- a/solution.py
+++ b/solution.py
@@ -299,15 +299,16 @@
         spots = pl.ds(pl.multiple_of(g * gcols, HD), gcols)
         oweights[g] = unpack_block(owords[:, spots])
 
-    for slot in range(slots):
-
-        @pl.when(takes[slot])
-        def _():
-            for j in range(2 * per_part):
-                halo_copy(slot, j).wait_recv()
-
     for head in range(local // HD):
         chunk, lanes = head // per_chunk, slice(head % per_chunk * HD, (head % per_chunk + 1) * HD)
+        if head % per_chunk == 0:
+            for slot in range(slots):
+
+                @pl.when(takes[slot])
+                def _():
+                    halo_copy(slot, chunk).wait_recv()
+                    halo_copy(slot, per_part + chunk).wait_recv()
+
         found, sums = gathered[head], totals[head]
         for slot in range(slots):
             more, more_sums = attend(

time: 54.3 us -> 52.9 us (0.974)
  Pallas kernels: 52.3 us -> 50.9 us
    pallas_call x1, Pallas kernels: 52.3 us -> 50.9 us  [on_device(): pl.pallas_call(functools.partial(layer_kernel, n, peers, distances, cols,...]
where the time goes in v2:
time: 52.9 us; the launch traced here: 52.8 us
  Pallas kernels  50.9 us (96%)
  local copies, waits for them, and re-layouts  1.84 us (3%)
    pallas_call x1, Pallas kernels, on_device(): pl.pallas_call(functools.partial(layer_kernel, n, peers, distances, cols,...  50.9 us
    unnamed x1, local copies, waits for them, and re-layouts  1.84 us

profile of v2, /device:TPU:0, one launch (start us, length us, event | category | flops | bytes accessed | tf_op | source)
XLA Modules:
  0.0 52.8 jit_solution(8551836788947365502)
XLA Ops:
  0.0 50.9 %layer.1 = bf16[48,5120]{1,0:T(8,128)(2,1)} custom-call(bf16[192,1280]{1,0:T(8,128)(2,1)} %bitcast.6, s32[5120]{0:T(1024)} %insigns_ref.1, f32[3,768]{1,0:T(4,128)} %qscale_ref.1, s32[3,768]{1,0:T(4,128)} %qsign_ref.1, s32[3,1,27]{2,1,0:T(1,128)} %bitcast.7, s32[768]{0:T(1024)} %osign_ref.1, f32[5120]{0:T(1024)} %oscale_ref.1, s32[5120]{0:T(1024)} %outsign_ref.1, ...), custom_call_target="tpu_custom_call" | custom-call | tf_op jit(solution)/shard_map/layer/pallas_call | solution.py:445
  50.9 1.8 %copy.16 = bf16[1,48,5120]{2,1,0:T(8,128)(2,1)} copy(bf16[1,48,5120]{2,1,0:T(8,128)(2,1)} %bitcast.5) | data formatting | bytes 983040
